TPU v7x, 32 devices: a whole 2x2x4 slice. The times are simulated.
32 devices in a mesh: sens: 4 (over y, x), slab: 8 (over z, core).
Axes of the slice: x: 2, y: 2, z: 4, core: 2. Of those that a mesh axis runs over, the one named last changes fastest.
Arguments:
- pressure: bfloat16 [32768, 128], P('slab'), may hold values from 0 to 1
- kernels: bfloat16 [4, 64, 256], replicated, may hold values from -0.0625 to 0.0625
- filter_gains: float32 [512], replicated, may hold values from 0.25 to 2
- measured: float32 [1024, 2, 512], P('sens'), may hold values from -6 to 6
- blocks: int32 [1024, 8, 64], P('sens', 'slab'), may hold values from 0 to 4095
- frames: int32 [1024, 8, 64], P('sens', 'slab'), may hold values from 0 to 2
- classes: int32 [1024, 8, 64], P('sens', 'slab'), may hold values from 0 to 3
- counts: int32 [1024, 8], P('sens', 'slab'), may hold values from 1 to 64, as said below
Outputs:
- residual: float32 [1024, 2, 512], P(('sens', 'slab'))
- gradient: float32 [32768, 128], P('slab', 'sens')
Inputs may be any that keep to these rules, and one draw needn't show every extreme that they name: counts[s, j] slots of sensor s in slab j are live; some sensor has all 64 slots live in some slab. `blocks`: slots at or past counts[s, j] are ignored.
All inputs are finite; a program needn't handle non-finite values.
Results may differ from a plain program's by a relative error of at most 0.00077.
Values may be sent and summed in bfloat16 or wider, within the bound.
No kernel may reach another device: no remote copies, remote signals or barrier semaphores. Data moves between devices by JAX's collectives and lax.ppermute only.
A program may use at most 256 MiB of HBM per device.

v0:
```python
import math
import jax
import jax.numpy as jnp
from jax import lax
from jax.sharding import PartitionSpec as P


def dft_pair(time_len):
    sample_ids = jnp.arange(time_len, dtype=jnp.int32)
    phase_ids = sample_ids[:, None] * sample_ids[None, :] % time_len
    angles = phase_ids.astype(jnp.float32) * (2.0 * math.pi / time_len)
    return (jnp.cos(angles), jnp.sin(angles))


def time_filter(traces, filter_gains, forward_basis, inverse_basis):
    time_len = filter_gains.shape[0]
    rows_flat = traces.reshape(-1, time_len)
    spectrum = jnp.dot(
        rows_flat,
        forward_basis,
        precision=lax.Precision.HIGHEST,
        preferred_element_type=jnp.float32,
    )
    spectrum = spectrum * jnp.concatenate([filter_gains, filter_gains])
    result = jnp.dot(
        spectrum, inverse_basis, precision=lax.Precision.HIGHEST, preferred_element_type=jnp.float32
    )
    return (result / time_len).reshape(traces.shape)


def per_device(pressure, kernels, filter_gains, measured, blocks, frames, classes, counts):
    kind_count, voxel_count, tap_count = kernels.shape
    block_count = pressure.shape[0]
    wave_count = pressure.shape[1] // voxel_count
    frame_len = tap_count // 2
    time_len = filter_gains.shape[0]
    frame_count = time_len // frame_len
    place_count = frame_count - 1
    combo_count = kind_count * place_count
    sensor_count, slot_count = (blocks.shape[0], blocks.shape[2])
    share_rows = sensor_count // lax.axis_size("slab")
    cosine_table, sine_table = dft_pair(time_len)
    forward_basis = jnp.concatenate([cosine_table, sine_table], axis=1)
    inverse_basis = jnp.concatenate([cosine_table, sine_table], axis=0)
    placed_list = []
    for offset in range(place_count):
        placed_list.append(
            jnp.pad(
                kernels,
                ((0, 0), (0, 0), (offset * frame_len, time_len - tap_count - offset * frame_len)),
            )
        )
    placed_kern = jnp.stack(placed_list, axis=1).reshape(combo_count, voxel_count, time_len)
    placed_wide = placed_kern.astype(jnp.float32)
    block_ids = blocks[:, 0, :]
    combo_ids = classes[:, 0, :] * place_count + frames[:, 0, :]
    live_slot = jnp.arange(slot_count, dtype=jnp.int32)[None, :] < counts[:, 0][:, None]
    combo_hot = (
        (combo_ids[:, :, None] == jnp.arange(combo_count, dtype=jnp.int32)) & live_slot[:, :, None]
    ).astype(jnp.bfloat16)
    block_range = jnp.arange(block_count, dtype=jnp.int32)
    picked_ids = block_ids.reshape(-1)
    row_hot = combo_hot
    picked = pressure[picked_ids].reshape(
        share_rows * lax.axis_size("slab"), slot_count, wave_count * voxel_count
    )
    grouped = jnp.einsum("skc,skx->scx", row_hot, picked, preferred_element_type=jnp.float32)
    grouped = grouped.reshape(
        share_rows * lax.axis_size("slab"), combo_count, wave_count, voxel_count
    )
    traces = lax.psum_scatter(
        jnp.einsum(
            "scwv,cvt->swt",
            grouped,
            placed_wide,
            precision=lax.Precision.HIGHEST,
            preferred_element_type=jnp.float32,
        ),
        "slab",
        scatter_dimension=0,
        tiled=True,
    )
    measured_share = lax.dynamic_slice_in_dim(
        measured, lax.axis_index("slab") * share_rows, share_rows, 0
    )
    residual = time_filter(traces, filter_gains, forward_basis, inverse_basis) - measured_share
    back_share = time_filter(residual, filter_gains, forward_basis, inverse_basis).astype(
        jnp.bfloat16
    )
    piece_rows = lax.all_gather(back_share, "slab", axis=0, tiled=True)
    row_count = piece_rows.shape[0]
    row_hot = combo_hot
    responses = jnp.einsum(
        "swt,cvt->scwv", piece_rows, placed_kern, preferred_element_type=jnp.float32
    )
    responses = responses.reshape(row_count * combo_count, wave_count * voxel_count)
    block_hot = (block_ids[:, :, None] == block_range).astype(jnp.bfloat16)
    tallies = jnp.einsum("skb,skc->bsc", block_hot, row_hot, preferred_element_type=jnp.float32)
    tallies = tallies.reshape(block_count, row_count * combo_count)
    partial_grad = jnp.dot(
        tallies, responses, precision=lax.Precision.HIGHEST, preferred_element_type=jnp.float32
    )
    gradient = lax.psum_scatter(partial_grad, "sens", scatter_dimension=1, tiled=True)
    return (residual, gradient)


def solution(mesh):
    return jax.shard_map(
        per_device,
        mesh=mesh,
        in_specs=(
            P("slab", None),
            P(),
            P(),
            P("sens", None, None),
            P("sens", "slab", None),
            P("sens", "slab", None),
            P("sens", "slab", None),
            P("sens", "slab"),
        ),
        out_specs=(P(("sens", "slab"), None, None), P("slab", "sens")),
        check_vma=False,
    )
```

profile of v0, /device:TPU:0, one launch (start us, length us, event | category | flops | bytes accessed | tf_op | source)
XLA Modules:
  0.0 294.1 jit_solution(7339451144219462057)
XLA Ops:
  7.2 0.9 iota_compare_fusion.5
  8.1 0.9 add_bitcast_fusion
  9.1 0.9 copy.16
  10.2 1.1 pad_bitcast_fusion.2
  11.5 0.9 copy.18
  12.4 57.4 %gather_fusion = bf16[16384,128]{1,0:T(8,128)(2,1)} fusion(bf16[4096,128]{1,0:T(8,128)(2,1)S(1)} %copy-done, s32[16384]{0:T(1024)S(1)} %broadcast_clamp_fusion), kind=kCustom, calls=%fused_computation | custom fusion | bytes 8454144 | tf_op jit(solution)/shard_map/gather | solution.py:64
  69.8 3.4 %fusion.5 = f32[256,12,128]{2,1,0:T(8,128)S(1)} fusion(bf16[256,64,128]{2,1,0:T(8,128)(2,1)} %bitcast.41, s32[256,64]{1,0:T(8,128)S(1)} %copy.15, pred[256,64]{1,0:T(8,128)(4,1)S(1)} %iota_compare_fusion.5), kind=kOutput, calls=%fused_computation.9 | convolution fusion | flops 50724864 | bytes 5849088 | tf_op jit(solution)/shard_map/skc,skx->scx/dot_general | solution.py:67
  73.2 1.6 copy.17
  74.8 3.8 %convolution_bitcast_fusion.1 = f32[256,2,512]{2,0,1:T(8,128)} fusion(f32[256,12,2,64]{0,3,2,1:T(8,128)} %bitcast.44, bf16[12,64,512,1]{2,1,3,0:T(8,128)(2,1)S(1)} %bitcast.42), kind=kOutput, calls=%fused_computation.18 | convolution fusion | flops 2415919104 | bytes 3407872 | tf_op jit(solution)/shard_map/scwv,cvt->swt/dot_general | solution.py:72
  78.9 46.5 %fusion.2 = f32[4096,256,12]{0,2,1:T(8,128)} fusion(s32[256,64]{1,0:T(8,128)S(1)} %copy.21, s32[256,64]{1,0:T(8,128)S(1)} %copy.15, pred[256,64]{1,0:T(8,128)(4,1)S(1)} %iota_compare_fusion.5), kind=kOutput, calls=%fused_computation.4 | convolution fusion | flops 1678114816 | bytes 50479104 | tf_op jit(solution)/shard_map/skb,skc->bsc/dot_general | solution.py:98
  125.4 54.3 %reshape.100 = f32[4096,3072]{0,1:T(8,128)} reshape(f32[4096,256,12]{0,2,1:T(8,128)} %fusion.2) | data formatting | bytes 100663296 | tf_op jit(solution)/shard_map/reshape | solution.py:99
  179.6 4.1 %fusion.27 = (f32[512,512]{1,0:T(8,128)S(1)}, f32[512,512]{1,0:T(8,128)S(1)}) fusion(), kind=kLoop, calls=%fused_computation.36 | loop fusion | flops 3670016 | bytes 2097152 | tf_op jit(solution)/shard_map/sin | solution.py:12
  183.8 1.0 copy.20
  184.9 1.4 fusion.11
  186.2 1.4 fusion.13
  187.7 1.0 dynamic-slice_subtract_fusion
  188.8 1.4 fusion.12
  190.2 1.4 fusion.15
  191.6 16.6 %all_gather.3 = bf16[256,2,512]{2,0,1:T(8,128)(2,1)S(1)} all-gather(bf16[32,2,512]{2,0,1:T(8,128)(2,1)S(1)} %copy.22), channel_id=1, replica_groups=mesh['sens'=4,'slab'=8] {'slab'}, dimensions={0}, use_global_device_ids=true | all-gather | bytes 589824 | tf_op jit(solution)/shard_map/all_gather | solution.py:90
  208.2 0.6 convolution_bitcast_fusion
  208.8 3.7 %copy.23 = f32[256,12,2,64]{3,2,1,0:T(2,128)} copy(f32[256,12,2,64]{0,3,2,1:T(8,128)S(1)} %convolution_bitcast_fusion) | data formatting | bytes 3145728 | tf_op jit(solution)/shard_map/swt,cvt->scwv/transpose | solution.py:93
  212.6 3.4 %reshape.102 = f32[3072,128]{1,0:T(8,128)S(1)} reshape(f32[256,12,2,64]{3,2,1,0:T(2,128)} %copy.23) | data formatting | bytes 3145728 | tf_op jit(solution)/shard_map/reshape | solution.py:96
  216.0 34.9 %fusion.33 = f32[4096,128]{0,1:T(8,128)} fusion(f32[4096,3072]{0,1:T(8,128)} %reshape.100, f32[3072,128]{1,0:T(8,128)S(1)} %reshape.102), kind=kOutput, calls=%fused_computation.51 | convolution fusion | flops 19327352832 | bytes 54001664 | tf_op jit(solution)/shard_map/dot_general | solution.py:100
  250.9 36.4 %reduce-scatter.5.cloned.1.call-done = f32[4096,32]{0,1:T(8,128)} async-done(((f32[4096,128]{0,1:T(8,128)}), f32[4096,32]{0,1:T(8,128)}) %reduce-scatter.5.cloned.1.call-update) | async-done | bytes 524304 | tf_op jit(solution)/shard_map/reduce_scatter | solution.py:103
  (31 shorter events, 1.0 us)
Async XLA Ops:
  7.2 5.2 %copy-start = (bf16[4096,128]{1,0:T(8,128)(2,1)S(1)}, bf16[4096,128]{1,0:T(8,128)(2,1)}, u32[]{:S(2)}) copy-start(bf16[4096,128]{1,0:T(8,128)(2,1)} %param.8) | copy-start | bytes 3145732
  7.2 176.6 %reduce-scatter.3.cloned.1.call-start = ((), (), s32[]{:S(2)}) async-start(), calls=%async_computation.2 | async-start | bytes 1179648 | tf_op jit(solution)/shard_map/reduce_scatter | solution.py:71
  73.2 1.6 copy-start.2
  74.8 3.9 %copy-start.5 = (s32[256,1,64]{0,2,1:T(8,128)S(1)}, s32[256,1,64]{0,2,1:T(8,128)}, u32[]{:S(2)}) copy-start(s32[256,1,64]{0,2,1:T(8,128)} %param.12) | copy-start | bytes 196612
  78.7 208.6 %reduce-scatter.5.cloned.1.call-start = ((), (), s32[]{:S(2)}) async-start(), calls=%async_computation.3 | async-start | bytes 2621440 | tf_op jit(solution)/shard_map/reduce_scatter | solution.py:103
  125.4 54.3 %copy-start.6 = (f32[512]{0:T(512)S(1)}, f32[512]{0:T(512)}, u32[]{:S(2)}) copy-start(f32[512]{0:T(512)} %param.10) | copy-start | bytes 6148
  188.7 2.9 copy-start.4
  190.2 18.0 %copy-start.3 = (bf16[4,3,64,512]{3,2,1,0:T(8,128)(2,1)S(1)}, bf16[4,3,64,512]{3,2,1,0:T(8,128)(2,1)}, u32[]{:S(2)}) copy-start(bf16[4,3,64,512]{3,2,1,0:T(8,128)(2,1)} %copy.18) | copy-start | bytes 2359300
  215.9 71.3 %copy-start.1 = (bf16[4096,128]{1,0:T(8,128)(2,1)S(1)}, bf16[4096,128]{1,0:T(8,128)(2,1)}, u32[]{:S(2)}) copy-start(bf16[4096,128]{1,0:T(8,128)(2,1)} %param.8) | copy-start | bytes 3145732
Sparse Core Ops, SparseCore 0:
  78.8 34.8 reduce-scatter.2
  251.0 36.1 reduce-scatter.4
where the time goes:
time: 295 us; the launch traced here: 294 us
  local copies, waits for them, and re-layouts  125 us (42%)
  matrix products  94.8 us (32%)
  waiting for transfers between devices  36.4 us (12%)
  blocking collectives  16.6 us (6%)
  between operations  14.2 us (5%)
  other arithmetic  6.99 us (2%)
    gather x1, local copies, waits for them, and re-layouts, per_device(): pressure[picked_ids]  57.4 us
    reshape x1, local copies, waits for them, and re-layouts, per_device(): tallies = tallies.reshape(block_count, row_count * combo_count)  54.3 us
    dot_general x1, matrix products, per_device(): jnp.einsum('skb,skc->bsc', block_hot, row_hot, preferred_element_type=jnp...  46.5 us
    reduce_scatter x1, waiting for transfers between devices, per_device(): lax.psum_scatter(partial_grad, 'sens', scatter_dimension=1, tiled=True)  36.4 us
    dot_general x1, matrix products, per_device(): jnp.dot(tallies, responses, precision=lax.Precision.HIGHEST, preferred_el...  34.9 us
    all_gather x1, blocking collectives, per_device(): piece_rows = lax.all_gather(back_share, 'slab', axis=0, tiled=True)  16.6 us
  transfers between devices with their start and end apart: 2, of which 1 were waited for; matrix products, arithmetic and copies ran while one was open for 36% of the time, Pallas kernels for 0%

commit v1 on v0

--- a/solution.py
+++ b/solution.py
@@ -3,6 +3,18 @@
 import jax.numpy as jnp
 from jax import lax
 from jax.sharding import PartitionSpec as P
+
+
+def collect(array, axis, dim):
+    ways, here, step = (lax.axis_size(axis), lax.axis_index(axis), array.shape[dim])
+    dims = [n * ways if d == dim else n for d, n in enumerate(array.shape)]
+    full = lax.dynamic_update_slice_in_dim(
+        jnp.zeros(dims, array.dtype), array, here * step, axis=dim
+    )
+    for far in range(1, ways):
+        array = lax.ppermute(array, axis, [(d, (d + 1) % ways) for d in range(ways)])
+        full = lax.dynamic_update_slice_in_dim(full, array, (here - far) % ways * step, axis=dim)
+    return full
 
 
 def dft_pair(time_len):
@@ -87,7 +99,7 @@
     back_share = time_filter(residual, filter_gains, forward_basis, inverse_basis).astype(
         jnp.bfloat16
     )
-    piece_rows = lax.all_gather(back_share, "slab", axis=0, tiled=True)
+    piece_rows = collect(back_share, "slab", 0)
     row_count = piece_rows.shape[0]
     row_hot = combo_hot
     responses = jnp.einsum(

time: 295 us -> 340 us (1.15)
  waiting for transfers between devices: 36.4 us -> 97.2 us
  blocking collectives: 16.6 us -> 0 us
    ppermute x0 -> x7, waiting for transfers between devices: none -> 32.8 us  [collect(): lax.ppermute(array, axis, [(d, (d + 1) % ways) for d in range(ways)])]
    reduce_scatter x1, waiting for transfers between devices: 0.02 us -> 30.7 us  [per_device(): lax.psum_scatter(jnp.einsum('scwv,cvt->swt', grouped, placed_wide, precis...]
    all_gather x1 -> x0, blocking collectives: 16.6 us -> none  [per_device(): piece_rows = lax.all_gather(back_share, 'slab', axis=0, tiled=True)]
  transfers between devices with their start and end apart: 2 -> 9, of which waited for: 1 -> 8; matrix products, arithmetic and copies ran while one was open for 36% -> 31% of each run, Pallas kernels for 0% -> 0%
where the time goes in v1:
time: 340 us; the launch traced here: 339 us
  local copies, waits for them, and re-layouts  125 us (37%)
  waiting for transfers between devices  97.2 us (29%)
  matrix products  94.8 us (28%)
  between operations  14.3 us (4%)
  other arithmetic  7 us (2%)
    gather x1, local copies, waits for them, and re-layouts, per_device(): pressure[picked_ids]  57.4 us
    reshape x1, local copies, waits for them, and re-layouts, per_device(): tallies = tallies.reshape(block_count, row_count * combo_count)  54.3 us
    dot_general x1, matrix products, per_device(): jnp.einsum('skb,skc->bsc', block_hot, row_hot, preferred_element_type=jnp...  46.5 us
    dot_general x1, matrix products, per_device(): jnp.dot(tallies, responses, precision=lax.Precision.HIGHEST, preferred_el...  35 us
    reduce_scatter x1, waiting for transfers between devices, per_device(): lax.psum_scatter(partial_grad, 'sens', scatter_dimension=1, tiled=True)  33.6 us
    ppermute x7, waiting for transfers between devices, collect(): lax.ppermute(array, axis, [(d, (d + 1) % ways) for d in range(ways)])  32.8 us
    reduce_scatter x1, waiting for transfers between devices, per_device(): lax.psum_scatter(jnp.einsum('scwv,cvt->swt', grouped, placed_wide, precis...  30.7 us
  transfers between devices with their start and end apart: 9, of which 8 were waited for; matrix products, arithmetic and copies ran while one was open for 31% of the time, Pallas kernels for 0%

profile of v1, /device:TPU:0, one launch (start us, length us, event | category | flops | bytes accessed | tf_op | source)
XLA Modules:
  0.0 338.8 jit_solution(4953304172154507191)
XLA Ops:
  10.3 1.1 pad_bitcast_fusion.2
  12.4 57.4 %gather_fusion = bf16[16384,128]{1,0:T(8,128)(2,1)} fusion(bf16[4096,128]{1,0:T(8,128)(2,1)S(1)} %copy-done, s32[16384]{0:T(1024)S(1)} %broadcast_clamp_fusion), kind=kCustom, calls=%fused_computation | custom fusion | bytes 8454144 | tf_op jit(solution)/shard_map/gather | solution.py:76
  69.8 3.4 fusion.5
  73.2 1.6 copy.18
  74.8 3.9 %convolution_bitcast_fusion.1 = f32[256,2,512]{2,0,1:T(8,128)} fusion(f32[256,12,2,64]{0,3,2,1:T(8,128)} %bitcast.44, bf16[12,64,512,1]{2,1,3,0:T(8,128)(2,1)S(1)} %bitcast.42), kind=kOutput, calls=%fused_computation.18 | convolution fusion | flops 2415919104 | bytes 3407872 | tf_op jit(solution)/shard_map/scwv,cvt->swt/dot_general | solution.py:84
  79.1 4.1 %fusion.27 = (f32[512,512]{1,0:T(8,128)S(1)}, f32[512,512]{1,0:T(8,128)S(1)}) fusion(), kind=kLoop, calls=%fused_computation.36 | loop fusion | flops 3670016 | bytes 2097152 | tf_op jit(solution)/shard_map/sin | solution.py:24
  83.2 30.7 %reduce-scatter.3.cloned.1.call-done = f32[32,2,512]{2,0,1:T(8,128)} async-done(((f32[256,2,512]{2,0,1:T(8,128)}), f32[32,2,512]{2,0,1:T(8,128)}) %reduce-scatter.3.cloned.1.call-update) | async-done | bytes 131088 | tf_op jit(solution)/shard_map/reduce_scatter | solution.py:83
  113.9 1.0 copy.21
  115.0 1.4 fusion.11
  116.4 1.4 fusion.13
  119.0 1.4 fusion.12
  120.3 1.4 fusion.15
  122.1 46.5 %fusion.2 = f32[4096,256,12]{0,2,1:T(8,128)} fusion(s32[256,64]{1,0:T(8,128)S(1)} %copy.22, s32[256,64]{1,0:T(8,128)S(1)} %copy.16, pred[256,64]{1,0:T(8,128)(4,1)S(1)} %copy-done.6), kind=kOutput, calls=%fused_computation.4 | convolution fusion | flops 1678114816 | bytes 50479104 | tf_op jit(solution)/shard_map/skb,skc->bsc/dot_general | solution.py:110
  168.6 54.3 %reshape.100 = f32[4096,3072]{0,1:T(8,128)} reshape(f32[4096,256,12]{0,2,1:T(8,128)} %fusion.2) | data formatting | bytes 100663296 | tf_op jit(solution)/shard_map/reshape | solution.py:111
  223.0 5.5 %collective-permute-done.1 = bf16[32,2,512]{2,0,1:T(8,128)(2,1)S(1)} collective-permute-done((bf16[32,2,512]{2,0,1:T(8,128)(2,1)S(1)}, bf16[32,2,512]{2,0,1:T(8,128)(2,1)S(1)}, u32[]{:S(2)}, u32[]{:S(2)}) %collective-permute-start.1) | collective-permute-done | bytes 65568 | tf_op jit(solution)/shard_map/ppermute | solution.py:15
  228.5 5.5 %collective-permute-done.2 = bf16[32,2,512]{2,0,1:T(8,128)(2,1)S(1)} collective-permute-done((bf16[32,2,512]{2,0,1:T(8,128)(2,1)S(1)}, bf16[32,2,512]{2,0,1:T(8,128)(2,1)S(1)}, u32[]{:S(2)}, u32[]{:S(2)}) %collective-permute-start.2) | collective-permute-done | bytes 65568 | tf_op jit(solution)/shard_map/ppermute | solution.py:15
  233.9 5.5 %collective-permute-done.3 = bf16[32,2,512]{2,0,1:T(8,128)(2,1)S(1)} collective-permute-done((bf16[32,2,512]{2,0,1:T(8,128)(2,1)S(1)}, bf16[32,2,512]{2,0,1:T(8,128)(2,1)S(1)}, u32[]{:S(2)}, u32[]{:S(2)}) %collective-permute-start.3) | collective-permute-done | bytes 65568 | tf_op jit(solution)/shard_map/ppermute | solution.py:15
  239.4 5.5 %collective-permute-done.4 = bf16[32,2,512]{2,0,1:T(8,128)(2,1)S(1)} collective-permute-done((bf16[32,2,512]{2,0,1:T(8,128)(2,1)S(1)}, bf16[32,2,512]{2,0,1:T(8,128)(2,1)S(1)}, u32[]{:S(2)}, u32[]{:S(2)}) %collective-permute-start.4) | collective-permute-done | bytes 65568 | tf_op jit(solution)/shard_map/ppermute | solution.py:15
  244.9 5.5 %collective-permute-done.5 = bf16[32,2,512]{2,0,1:T(8,128)(2,1)S(1)} collective-permute-done((bf16[32,2,512]{2,0,1:T(8,128)(2,1)S(1)}, bf16[32,2,512]{2,0,1:T(8,128)(2,1)S(1)}, u32[]{:S(2)}, u32[]{:S(2)}) %collective-permute-start.5) | collective-permute-done | bytes 65568 | tf_op jit(solution)/shard_map/ppermute | solution.py:15
  250.4 5.5 %collective-permute-done.6 = bf16[32,2,512]{2,0,1:T(8,128)(2,1)S(1)} collective-permute-done((bf16[32,2,512]{2,0,1:T(8,128)(2,1)S(1)}, bf16[32,2,512]{2,0,1:T(8,128)(2,1)S(1)}, u32[]{:S(2)}, u32[]{:S(2)}) %collective-permute-start.6) | collective-permute-done | bytes 65568 | tf_op jit(solution)/shard_map/ppermute | solution.py:15
  256.5 3.5 %copy.25 = f32[256,12,2,64]{3,2,1,0:T(2,128)} copy(f32[256,12,2,64]{0,3,2,1:T(8,128)S(1)} %convolution_bitcast_fusion) | data formatting | bytes 3145728 | tf_op jit(solution)/shard_map/swt,cvt->scwv/transpose | solution.py:105
  260.0 3.4 reshape.102
  263.4 35.0 %fusion.34 = f32[4096,128]{0,1:T(8,128)} fusion(f32[4096,3072]{0,1:T(8,128)} %reshape.100, f32[3072,128]{1,0:T(8,128)S(1)} %reshape.102), kind=kOutput, calls=%fused_computation.60 | convolution fusion | flops 19327352832 | bytes 54001664 | tf_op jit(solution)/shard_map/dot_general | solution.py:112
  298.4 33.6 %reduce-scatter.5.cloned.1.call-done = f32[4096,32]{0,1:T(8,128)} async-done(((f32[4096,128]{0,1:T(8,128)}), f32[4096,32]{0,1:T(8,128)}) %reduce-scatter.5.cloned.1.call-update) | async-done | bytes 524304 | tf_op jit(solution)/shard_map/reduce_scatter | solution.py:115
  (56 shorter events, 6.7 us)
Async XLA Ops:
  7.2 5.3 %copy-start = (bf16[4096,128]{1,0:T(8,128)(2,1)S(1)}, bf16[4096,128]{1,0:T(8,128)(2,1)}, u32[]{:S(2)}) copy-start(bf16[4096,128]{1,0:T(8,128)(2,1)} %param.8) | copy-start | bytes 3145732
  7.2 106.7 %reduce-scatter.3.cloned.1.call-start = ((), (), s32[]{:S(2)}) async-start(), calls=%async_computation.2 | async-start | bytes 1179648 | tf_op jit(solution)/shard_map/reduce_scatter | solution.py:83
  8.1 61.7 %copy-start.5 = (pred[256,64]{1,0:T(8,128)(4,1)}, pred[256,64]{1,0:T(8,128)(4,1)S(1)}, u32[]{:S(2)}) copy-start(pred[256,64]{1,0:T(8,128)(4,1)S(1)} %iota_compare_fusion.5) | copy-start | bytes 49156
  73.2 1.6 copy-start.2
  74.8 4.1 %copy-start.7 = (s32[256,1,64]{0,2,1:T(8,128)S(1)}, s32[256,1,64]{0,2,1:T(8,128)}, u32[]{:S(2)}) copy-start(s32[256,1,64]{0,2,1:T(8,128)} %param.12) | copy-start | bytes 196612
  74.8 4.2 %copy-start.8 = (f32[512]{0:T(512)S(1)}, f32[512]{0:T(512)}, u32[]{:S(2)}) copy-start(f32[512]{0:T(512)} %param.10) | copy-start | bytes 6148
  78.7 253.2 %reduce-scatter.5.cloned.1.call-start = ((), (), s32[]{:S(2)}) async-start(), calls=%async_computation.3 | async-start | bytes 2621440 | tf_op jit(solution)/shard_map/reduce_scatter | solution.py:115
  118.8 2.9 copy-start.4
  120.3 1.8 copy-start.6
  121.8 101.1 %collective-permute-start = (bf16[32,2,512]{2,0,1:T(8,128)(2,1)S(1)}, bf16[32,2,512]{2,0,1:T(8,128)(2,1)S(1)}, u32[]{:S(2)}, u32[]{:S(2)}) collective-permute-start(bf16[32,2,512]{2,0,1:T(8,128)(2,1)S(1)} %get-tuple-element.5), channel_id=1, source_target_pairs={{0,1},{1,2},{2,3},{3,4},{4,5},{5,6},{6,7},{7,0},{8,9},{9,10},{10,1... | collective-permute-start | bytes 196616 | tf_op jit(solution)/shard_map/ppermute | solution.py:15
  168.6 87.3 %copy-start.3 = (bf16[4,3,64,512]{3,2,1,0:T(8,128)(2,1)S(1)}, bf16[4,3,64,512]{3,2,1,0:T(8,128)(2,1)}, u32[]{:S(2)}) copy-start(bf16[4,3,64,512]{3,2,1,0:T(8,128)(2,1)} %copy.19) | copy-start | bytes 2359300
  222.9 5.5 %collective-permute-start.1 = (bf16[32,2,512]{2,0,1:T(8,128)(2,1)S(1)}, bf16[32,2,512]{2,0,1:T(8,128)(2,1)S(1)}, u32[]{:S(2)}, u32[]{:S(2)}) collective-permute-start(bf16[32,2,512]{2,0,1:T(8,128)(2,1)S(1)} %collective-permute-done), channel_id=1, source_target_pairs={{0,1},{1,2},{2,3},{3,4},{4,5},{5,6},{6,7},{7,0},{8,9},{9,10},{10,1... | collective-permute-start | bytes 196616 | tf_op jit(solution)/shard_map/ppermute | solution.py:15
  228.4 5.5 %collective-permute-start.2 = (bf16[32,2,512]{2,0,1:T(8,128)(2,1)S(1)}, bf16[32,2,512]{2,0,1:T(8,128)(2,1)S(1)}, u32[]{:S(2)}, u32[]{:S(2)}) collective-permute-start(bf16[32,2,512]{2,0,1:T(8,128)(2,1)S(1)} %collective-permute-done.1), channel_id=1, source_target_pairs={{0,1},{1,2},{2,3},{3,4},{4,5},{5,6},{6,7},{7,0},{8,9},{9,10},{10,1... | collective-permute-start | bytes 196616 | tf_op jit(solution)/shard_map/ppermute | solution.py:15
  233.9 5.5 %collective-permute-start.3 = (bf16[32,2,512]{2,0,1:T(8,128)(2,1)S(1)}, bf16[32,2,512]{2,0,1:T(8,128)(2,1)S(1)}, u32[]{:S(2)}, u32[]{:S(2)}) collective-permute-start(bf16[32,2,512]{2,0,1:T(8,128)(2,1)S(1)} %collective-permute-done.2), channel_id=1, source_target_pairs={{0,1},{1,2},{2,3},{3,4},{4,5},{5,6},{6,7},{7,0},{8,9},{9,10},{10,1... | collective-permute-start | bytes 196616 | tf_op jit(solution)/shard_map/ppermute | solution.py:15
  239.4 5.5 %collective-permute-start.4 = (bf16[32,2,512]{2,0,1:T(8,128)(2,1)S(1)}, bf16[32,2,512]{2,0,1:T(8,128)(2,1)S(1)}, u32[]{:S(2)}, u32[]{:S(2)}) collective-permute-start(bf16[32,2,512]{2,0,1:T(8,128)(2,1)S(1)} %collective-permute-done.3), channel_id=1, source_target_pairs={{0,1},{1,2},{2,3},{3,4},{4,5},{5,6},{6,7},{7,0},{8,9},{9,10},{10,1... | collective-permute-start | bytes 196616 | tf_op jit(solution)/shard_map/ppermute | solution.py:15
  244.9 5.5 %collective-permute-start.5 = (bf16[32,2,512]{2,0,1:T(8,128)(2,1)S(1)}, bf16[32,2,512]{2,0,1:T(8,128)(2,1)S(1)}, u32[]{:S(2)}, u32[]{:S(2)}) collective-permute-start(bf16[32,2,512]{2,0,1:T(8,128)(2,1)S(1)} %collective-permute-done.4), channel_id=1, source_target_pairs={{0,1},{1,2},{2,3},{3,4},{4,5},{5,6},{6,7},{7,0},{8,9},{9,10},{10,1... | collective-permute-start | bytes 196616 | tf_op jit(solution)/shard_map/ppermute | solution.py:15
  250.4 5.5 %collective-permute-start.6 = (bf16[32,2,512]{2,0,1:T(8,128)(2,1)S(1)}, bf16[32,2,512]{2,0,1:T(8,128)(2,1)S(1)}, u32[]{:S(2)}, u32[]{:S(2)}) collective-permute-start(bf16[32,2,512]{2,0,1:T(8,128)(2,1)S(1)} %collective-permute-done.5), channel_id=1, source_target_pairs={{0,1},{1,2},{2,3},{3,4},{4,5},{5,6},{6,7},{7,0},{8,9},{9,10},{10,1... | collective-permute-start | bytes 196616 | tf_op jit(solution)/shard_map/ppermute | solution.py:15
  263.4 68.6 %copy-start.1 = (bf16[4096,128]{1,0:T(8,128)(2,1)S(1)}, bf16[4096,128]{1,0:T(8,128)(2,1)}, u32[]{:S(2)}) copy-start(bf16[4096,128]{1,0:T(8,128)(2,1)} %param.8) | copy-start | bytes 3145732
Sparse Core Ops, SparseCore 0:
  78.8 35.0 reduce-scatter.2
  298.5 33.4 reduce-scatter.4
